TPU v7x, 512 devices: a whole 4x4x16 slice. The times are simulated.
512 devices in a mesh: req: 8 (over x, core), vocab: 64 (over y, z).
Axes of the slice: x: 4, y: 4, z: 16, core: 2. Of those that a mesh axis runs over, the one named last changes fastest.
Arguments:
- hidden: bfloat16 [8192, 2304], P(('req', 'vocab'))
- norm_gain: float32 [2304], replicated, may hold values from 0.5 to 1.5
- head_weight: bfloat16 [2304, 65536], P(None, 'vocab')
- targets: int32 [8192], P(('req', 'vocab')), may hold values from 0 to 65535
- counts: int32 [512], P(('req', 'vocab')), may hold values from 5 to 10, as said below
Outputs:
- logprob: float32 [8192], P(('req', 'vocab'))
- entropy: float32 [8192], P(('req', 'vocab'))
Inputs may be any that keep to these rules, and one draw needn't show every extreme that they name: The scored slots of a device are its first counts slots; some device holds exactly 10.
All inputs are finite; a program needn't handle non-finite values.
Results may differ from a plain program's by a relative error of at most 0.012.
The roundings to bfloat16 on the way count: a program that leaves them out, or rounds other values in their place, can miss the bound.
Values may be sent and summed in bfloat16 or wider, within the bound.
A program may use at most 64 MiB of HBM per device.

v0:
```python
import jax
import jax.numpy as jnp
from jax import lax
from jax.sharding import PartitionSpec as P

logit_scale = 256.0 / 2304.0


def on_device(hidden, norm_gain, head_weight, targets, counts):
    slots = hidden.shape[0]
    vocab_dev = head_weight.shape[1]
    values = hidden.astype(jnp.float32)
    square_mean = jnp.mean(values * values, axis=1, keepdims=True)
    normed = (values * lax.rsqrt(square_mean + 1e-05) * norm_gain[None, :]).astype(jnp.bfloat16)
    gathered = lax.all_gather(normed, "vocab", axis=0, tiled=True)
    wanted = lax.all_gather(targets, "vocab", axis=0, tiled=True)
    position = lax.axis_index("vocab")
    start = position * vocab_dev
    logits = jnp.dot(gathered, head_weight, preferred_element_type=jnp.float32) * logit_scale
    local_peak = jnp.max(logits, axis=1)
    weights = jnp.exp(logits - local_peak[:, None])
    local_total = jnp.sum(weights, axis=1)
    local_moment = jnp.sum(weights * logits, axis=1)
    columns = lax.broadcasted_iota(jnp.int32, logits.shape, 1)
    hits = columns == (wanted - start)[:, None]
    local_chosen = jnp.sum(jnp.where(hits, logits, jnp.float32(0.0)), axis=1)
    own_start = position * slots
    peak = lax.pmax(local_peak, "vocab")
    factor = jnp.exp(local_peak - peak)
    total, moment, chosen = lax.psum(
        (local_total * factor, local_moment * factor, local_chosen), "vocab"
    )
    peak = lax.dynamic_slice_in_dim(peak, own_start, slots, 0)
    total = lax.dynamic_slice_in_dim(total, own_start, slots, 0)
    moment = lax.dynamic_slice_in_dim(moment, own_start, slots, 0)
    chosen = lax.dynamic_slice_in_dim(chosen, own_start, slots, 0)
    log_total = jnp.log(total)
    row_logprob = chosen - peak - log_total
    row_entropy = peak + log_total - moment / total
    scored = jnp.arange(slots, dtype=jnp.int32) < counts[0]
    logprob = jnp.where(scored, row_logprob, jnp.float32(0.0))
    entropy = jnp.where(scored, row_entropy, jnp.float32(0.0))
    return (logprob, entropy)


def solution(mesh):
    in_specs = (
        P(("req", "vocab"), None),
        P(),
        P(None, "vocab"),
        P(("req", "vocab")),
        P(("req", "vocab")),
    )
    out_specs = (P(("req", "vocab")), P(("req", "vocab")))
    return jax.shard_map(
        on_device, mesh=mesh, in_specs=in_specs, out_specs=out_specs, check_vma=False
    )
```

profile of v0, /device:TPU:2, one launch (start us, length us, event | category | flops | bytes accessed | tf_op | source)
XLA Modules:
  0.0 597.7 jit_solution(12411785864831970918)
XLA Ops:
  7.2 0.0 all-gather.2.cloned.1.call-start
  7.2 1.0 fusion.1
  8.2 1.6 fusion.3
  9.8 0.0 all-gather.2.cloned.1.call-update
  10.5 1.3 dynamic-slice
  12.5 0.9 dynamic-update-slice
  13.3 34.4 %all-reduce = s32[1024]{0:T(1024)S(1)} all-reduce(s32[1024]{0:T(1024)S(1)} %dynamic-update-slice), channel_id=1, replica_groups=mesh['req'=8,'vocab'=64] {'vocab'}, use_global_device_ids=true, to_apply=%add | all-reduce | flops 1024 | bytes 8192
  47.7 115.1 %all-gather.2.cloned.1.call-done = bf16[1024,2304]{1,0:T(8,128)(2,1)} async-done(((bf16[16,2304]{1,0:T(8,128)(2,1)}), bf16[1024,2304]{1,0:T(8,128)(2,1)}) %all-gather.2.cloned.1.call-update) | async-done | bytes 4718608 | tf_op jit(solution)/shard_map/all_gather | solution.py:15
  162.8 9.8 %multiply_reduce_fusion.1 = (f32[1024]{0:T(1024)S(1)}, f32[1024,1024]{0,1:T(8,128)}) fusion(bf16[1024,2304]{1,0:T(8,128)(2,1)} %all-gather.2.cloned.1.call-done, bf16[2304,1024]{1,0:T(8,128)(2,1)} %param.7), kind=kOutput, calls=%fused_computation.5 | convolution fusion | flops 4833934336 | bytes 13635584 | tf_op jit(solution)/shard_map/dot_general | solution.py:19
  172.6 140.0 %pmax.7 = f32[1024]{0:T(1024)S(1)} all-reduce(f32[1024]{0:T(1024)S(1)} %get-tuple-element.12), channel_id=1, replica_groups=mesh['req'=8,'vocab'=64] {'vocab'}, use_global_device_ids=true, to_apply=%region_4.5 | all-reduce | flops 1024 | bytes 8192 | tf_op jit(solution)/shard_map/pmax | solution.py:28
  312.6 3.7 multiply_reduce_fusion
  316.3 274.0 %all-reduce.1 = (f32[1024]{0:T(1024)S(1)}, f32[1024]{0:T(1024)S(1)}, f32[1024]{0:T(1024)S(1)}) all-reduce(f32[1024]{0:T(1024)S(1)} %get-tuple-element.4, f32[1024]{0:T(1024)S(1)} %get-tuple-element.11, f32[1024]{0:T(1024)S(1)} %get-tuple-element.10), channel_id=1, replica_groups=mesh['req'=8,'vocab'=64] {'vocab'}, use_global_device_ids=true, to_apply=%region_2.0 | all-reduce | flops 3072 | bytes 24576 | tf_op jit(solution)/shard_map/psum | solution.py:30
  590.3 0.6 compare_select_fusion
  (4 shorter events, 0.0 us)
Async XLA Ops:
  7.2 155.7 %all-gather.2.cloned.1.call-start = ((), (), s32[]{:S(2)}) async-start(), calls=%async_computation | async-start | bytes 4792320 | tf_op jit(solution)/shard_map/all_gather | solution.py:15
Sparse Core Ops, SparseCore 0:
  10.9 151.8 all-gather.1
where the time goes:
time: 598 us
  blocking collectives  448 us (75%)
  waiting for transfers between devices  115 us (19%)
  between operations  15.4 us (3%)
  matrix products  9.76 us (2%)
  other arithmetic  6.94 us (1%)
    psum x1, blocking collectives, on_device(): lax.psum((local_total * factor, local_moment * factor, local_chosen), 'vo...  274 us
    pmax x1, blocking collectives, on_device(): peak = lax.pmax(local_peak, 'vocab')  140 us
    all_gather x1, waiting for transfers between devices, on_device(): gathered = lax.all_gather(normed, 'vocab', axis=0, tiled=True)  115 us
    unnamed x1, blocking collectives  34.4 us
  transfers between devices with their start and end apart: 1, of which 1 were waited for; matrix products, arithmetic and copies ran while one was open for 0% of the time, Pallas kernels for 0%

commit v1 on v0

--- a/solution.py
+++ b/solution.py
@@ -12,7 +12,9 @@
     values = hidden.astype(jnp.float32)
     square_mean = jnp.mean(values * values, axis=1, keepdims=True)
     normed = (values * lax.rsqrt(square_mean + 1e-05) * norm_gain[None, :]).astype(jnp.bfloat16)
-    gathered = lax.all_gather(normed, "vocab", axis=0, tiled=True)
+    gathered = jnp.concatenate(
+        lax.all_to_all(jnp.stack([normed] * lax.axis_size("vocab")), "vocab", 0, 0), axis=0
+    )
     wanted = lax.all_gather(targets, "vocab", axis=0, tiled=True)
     position = lax.axis_index("vocab")
     start = position * vocab_dev

time: 598 us -> 678 us (1.13)
  the two profiles are of different devices: /device:TPU:2 before, /device:TPU:6 now
where the time goes in v1:
time: 678 us
  blocking collectives  637 us (94%)
  starting transfers between devices  19.1 us (3%)
  matrix products  9.77 us (1%)
    psum x1, blocking collectives, on_device(): lax.psum((local_total * factor, local_moment * factor, local_chosen), 'vo...  274 us
    unnamed x1, blocking collectives  222 us
    pmax x1, blocking collectives, on_device(): peak = lax.pmax(local_peak, 'vocab')  141 us
    all_to_all x1, starting transfers between devices, on_device(): lax.all_to_all(jnp.stack([normed] * lax.axis_size('vocab')), 'vocab', 0, 0)  19.1 us
  transfers between devices with their start and end apart: 1, of which 0 were waited for; matrix products, arithmetic and copies ran while one was open for 0% of the time, Pallas kernels for 0%

profile of v1, /device:TPU:6, one launch (start us, length us, event | category | flops | bytes accessed | tf_op | source)
XLA Modules:
  0.0 677.8 jit_solution(18378045166115038585)
XLA Ops:
  0.6 1.0 fusion.1
  1.7 1.0 fusion.3
  2.6 2.5 stack.2
  5.1 0.0 copy-start
  5.1 19.1 %all-to-all-start = ((bf16[64,16,2304]{2,1,0:T(8,128)(2,1)}), bf16[64,16,2304]{2,1,0:T(8,128)(2,1)}, u32[]{:S(2)}, u32[]{:S(2)}) async-start(bf16[64,16,2304]{2,1,0:T(8,128)(2,1)} %stack.2), calls=%async_computation | async-start | bytes 9437184 | tf_op jit(solution)/shard_map/all_to_all | solution.py:16
  24.9 1.3 dynamic-slice
  26.8 0.0 copy-done
  26.8 0.2 dynamic-update-slice
  27.1 221.6 %all-reduce = s32[1024]{0:T(1024)S(1)} all-reduce(s32[1024]{0:T(1024)S(1)} %dynamic-update-slice), channel_id=1, replica_groups=mesh['req'=8,'vocab'=64] {'vocab'}, use_global_device_ids=true, to_apply=%add | all-reduce | flops 1024 | bytes 8192
  248.6 0.0 all-to-all-done
  248.6 9.8 %multiply_reduce_fusion.1 = (f32[1024]{0:T(1024)S(1)}, f32[1024,1024]{0,1:T(8,128)}) fusion(bf16[1024,2304]{1,0:T(8,128)(2,1)} %bitcast.2, bf16[2304,1024]{1,0:T(8,128)(2,1)} %param.7), kind=kOutput, calls=%fused_computation.5 | convolution fusion | flops 4833934336 | bytes 13635584 | tf_op jit(solution)/shard_map/dot_general | solution.py:21
  258.4 141.1 %pmax.7 = f32[1024]{0:T(1024)S(1)} all-reduce(f32[1024]{0:T(1024)S(1)} %get-tuple-element.12), channel_id=1, replica_groups=mesh['req'=8,'vocab'=64] {'vocab'}, use_global_device_ids=true, to_apply=%region_4.5 | all-reduce | flops 1024 | bytes 8192 | tf_op jit(solution)/shard_map/pmax | solution.py:30
  399.5 3.7 multiply_reduce_fusion
  403.2 274.0 %all-reduce.1 = (f32[1024]{0:T(1024)S(1)}, f32[1024]{0:T(1024)S(1)}, f32[1024]{0:T(1024)S(1)}) all-reduce(f32[1024]{0:T(1024)S(1)} %get-tuple-element.4, f32[1024]{0:T(1024)S(1)} %get-tuple-element.11, f32[1024]{0:T(1024)S(1)} %get-tuple-element.10), channel_id=1, replica_groups=mesh['req'=8,'vocab'=64] {'vocab'}, use_global_device_ids=true, to_apply=%region_2.0 | all-reduce | flops 3072 | bytes 24576 | tf_op jit(solution)/shard_map/psum | solution.py:32
  677.2 0.6 compare_select_fusion
  (4 shorter events, 0.0 us)
Async XLA Ops:
  5.1 21.7 %copy-start = (s32[16]{0:T(128)S(1)}, s32[16]{0:T(128)}, u32[]{:S(2)}) copy-start(s32[16]{0:T(128)} %param.8) | copy-start | bytes 196
  5.1 243.5 %all-to-all-start = ((bf16[64,16,2304]{2,1,0:T(8,128)(2,1)}), bf16[64,16,2304]{2,1,0:T(8,128)(2,1)}, u32[]{:S(2)}, u32[]{:S(2)}) async-start(bf16[64,16,2304]{2,1,0:T(8,128)(2,1)} %stack.2), calls=%async_computation | async-start | bytes 9437184 | tf_op jit(solution)/shard_map/all_to_all | solution.py:16
